TPU v7x, 32 devices: a whole 2x2x4 slice. The times are simulated.
32 devices in a mesh: pages: 8 (over y, x, core), heads: 4 (over z).
Axes of the slice: x: 2, y: 2, z: 4, core: 2. Of those that a mesh axis runs over, the one named last changes fastest.
Arguments:
- hidden: bfloat16 [16, 608, 768], P('pages', 'heads'), may hold values from -6 to 6
- qkv_weight: bfloat16 [768, 3, 768], P(None, None, 'heads'), may hold values from -0.21875 to 0.21875
- qv_bias: bfloat16 [2, 768], P(None, 'heads'), may hold values from -3 to 3
- out_weight: bfloat16 [768, 768], P('heads'), may hold values from -0.875 to 0.875
- out_bias: bfloat16 [768], replicated, may hold values from -2 to 2
- first_gain: bfloat16 [768], replicated, may hold values from 0.5 to 1.5
- first_shift: bfloat16 [768], replicated, may hold values from -2 to 2
- up_weight: bfloat16 [768, 3072], P(None, 'heads'), may hold values from -0.21875 to 0.21875
- up_bias: bfloat16 [3072], P('heads'), may hold values from -2 to 2
- down_weight: bfloat16 [3072, 768], P('heads'), may hold values from -0.15625 to 0.15625
- down_bias: bfloat16 [768], replicated, may hold values from -2 to 2
- second_gain: bfloat16 [768], replicated, may hold values from 0.5 to 1.5
- second_shift: bfloat16 [768], replicated, may hold values from -2 to 2
- relative_table: bfloat16 [32, 12], P(None, 'heads'), may hold values from -4 to 4
- horizontal_table: bfloat16 [64, 12], P(None, 'heads'), may hold values from -4 to 4
- vertical_table: bfloat16 [64, 12], P(None, 'heads'), may hold values from -4 to 4
- token_mask: int32 [16, 608], P('pages'), may hold values from 0 to 1, as said below
- relative_ids: int32 [16, 608, 608], P('pages'), may hold values from 0 to 31
- horizontal_ids: int32 [16, 608, 608], P('pages'), may hold values from 0 to 63
- vertical_ids: int32 [16, 608, 608], P('pages'), may hold values from 0 to 63
- cotangent: bfloat16 [16, 608, 768], P('pages', 'heads'), may hold values from -18 to 18
Outputs:
- output: bfloat16 [16, 608, 768], P('pages', 'heads')
- grad_hidden: bfloat16 [16, 608, 768], P('pages', 'heads')
- grad_qkv_weight: float32 [768, 3, 768], P(None, None, 'heads')
- grad_qv_bias: float32 [2, 768], P(None, 'heads')
- grad_out_weight: float32 [768, 768], P('heads')
- grad_out_bias: float32 [768], replicated
- grad_first_gain: float32 [768], replicated
- grad_first_shift: float32 [768], replicated
- grad_up_weight: float32 [768, 3072], P(None, 'heads')
- grad_up_bias: float32 [3072], P('heads')
- grad_down_weight: float32 [3072, 768], P('heads')
- grad_down_bias: float32 [768], replicated
- grad_second_gain: float32 [768], replicated
- grad_second_shift: float32 [768], replicated
- grad_relative_table: float32 [32, 12], P(None, 'heads')
- grad_horizontal_table: float32 [64, 12], P(None, 'heads')
- grad_vertical_table: float32 [64, 12], P(None, 'heads')
Inputs may be any that keep to these rules, and one draw needn't show every extreme that they name: `token_mask`: ones mark real tokens: in each page the text tokens fill positions 0 to L - 1, with L from 40 to 512, and the visual tokens positions 512 to 560; every draw has a page with L = 512 and one with L = 40.
All inputs are finite; a program needn't handle non-finite values.
Results may differ from a plain program's by a relative error of at most 0.02.
Values may be sent and summed in bfloat16 or wider, within the bound.
A program may use at most 192 MiB of HBM per device.

v0:
```python
from functools import partial

import jax
import jax.numpy as jnp
from jax import lax
from jax.sharding import PartitionSpec as P

bias_parts = 8


def layer_norm(value, gain, shift):
    middle = jnp.mean(value, axis=-1, keepdims=True)
    centred = value - middle
    spread = jnp.mean(centred * centred, axis=-1, keepdims=True)
    return centred * lax.rsqrt(spread + 1e-12) * gain + shift


def bucket_onehot(ids_piece, buckets):
    levels = lax.broadcasted_iota(jnp.int32, (buckets, ids_piece.shape[1]), 0)
    matches = (
        (ids_piece[0][None, :] == levels)
        | (ids_piece[1][None, :] == levels)
        | (ids_piece[2][None, :] == levels)
    )
    return matches.astype(jnp.bfloat16)


def split_pairs(array):
    leading, seq_len = (array.shape[0], array.shape[1])
    per_part = seq_len * seq_len // bias_parts
    return jnp.transpose(array.reshape(leading, bias_parts, per_part), (1, 0, 2))


def page_bias(ids_three, table_all):
    heads_here, buckets = table_all.shape
    seq_len = ids_three.shape[1]

    def one_part(ids_piece):
        return jnp.dot(
            table_all, bucket_onehot(ids_piece, buckets), preferred_element_type=jnp.float32
        )

    parts_out = lax.map(one_part, split_pairs(ids_three))
    return jnp.transpose(parts_out, (1, 0, 2)).reshape(heads_here, seq_len, seq_len)


def table_grad(ids_three, grad_scores, buckets):
    heads_here = grad_scores.shape[0]

    def add_part(running, paired):
        ids_piece, grad_piece = paired
        onehot = bucket_onehot(ids_piece, buckets)
        term = lax.dot_general(
            onehot, grad_piece, (((1,), (1,)), ((), ())), preferred_element_type=jnp.float32
        )
        return (running + term, None)

    start = jnp.zeros((buckets, heads_here), jnp.float32)
    running, unused = lax.scan(add_part, start, (split_pairs(ids_three), split_pairs(grad_scores)))
    return running


def page_scores(queries, keys_all, valid, bias):
    scores = (
        jnp.einsum("qhd,khd->hqk", queries, keys_all, preferred_element_type=jnp.float32) * 0.125
        + bias
    )
    return jnp.where(valid[None, None, :] > 0, scores, -1000000000.0)


def page_forward(queries, keys_all, values_all, valid, ids_three, table_all):
    bias = page_bias(ids_three, table_all)
    scores = page_scores(queries, keys_all, valid, bias)
    row_max = jnp.max(scores, axis=-1, keepdims=True)
    summed = jnp.sum(jnp.exp(scores - row_max), axis=-1, keepdims=True)
    log_total = row_max + jnp.log(summed)
    probs_low = jnp.exp(scores - log_total).astype(jnp.bfloat16)
    attended = jnp.einsum("hqk,khd->qhd", probs_low, values_all, preferred_element_type=jnp.float32)
    return (attended.astype(jnp.bfloat16), log_total, bias)


def page_backward(
    queries, keys_all, values_all, valid, ids_three, log_total, bias, grad_att, table_all
):
    scores = page_scores(queries, keys_all, valid, bias)
    probs = jnp.exp(scores - log_total)
    probs_low = probs.astype(jnp.bfloat16)
    grad_values = jnp.einsum(
        "hqk,qhd->khd", probs_low, grad_att, preferred_element_type=jnp.float32
    )
    grad_probs = jnp.einsum(
        "qhd,khd->hqk", grad_att, values_all, preferred_element_type=jnp.float32
    )
    inner = jnp.sum(probs * grad_probs, axis=-1, keepdims=True)
    grad_scores = (probs * (grad_probs - inner)).astype(jnp.bfloat16)
    grad_queries = (
        jnp.einsum("hqk,khd->qhd", grad_scores, keys_all, preferred_element_type=jnp.float32)
        * 0.125
    )
    grad_keys = (
        jnp.einsum("hqk,qhd->khd", grad_scores, queries, preferred_element_type=jnp.float32) * 0.125
    )
    grad_tables = table_grad(ids_three, grad_scores, table_all.shape[1])
    return (grad_queries, grad_keys, grad_values, grad_tables)


def shards(
    hidden,
    qkv_weight,
    qv_bias,
    out_weight,
    out_bias,
    first_gain,
    first_shift,
    up_weight,
    up_bias,
    down_weight,
    down_bias,
    second_gain,
    second_shift,
    relative_table,
    horizontal_table,
    vertical_table,
    token_mask,
    relative_ids,
    horizontal_ids,
    vertical_ids,
    cotangent,
):
    pages_here = hidden.shape[0]
    model_width = hidden.shape[2]
    seq_len = relative_ids.shape[1]
    heads_here = relative_table.shape[1]
    local_width = qkv_weight.shape[2]
    head_size = local_width // heads_here
    rel_count = relative_table.shape[0]
    pos_count = horizontal_table.shape[0]
    table_all = jnp.transpose(
        jnp.concatenate([relative_table, horizontal_table, vertical_table], axis=0)
    )
    ids_all = jnp.stack(
        [relative_ids, horizontal_ids + rel_count, vertical_ids + rel_count + pos_count], axis=1
    )
    gathered = lax.all_gather(hidden, "heads", axis=1, tiled=True)
    weight_flat = qkv_weight.reshape(model_width, 3 * local_width)
    projected = jnp.dot(gathered, weight_flat, preferred_element_type=jnp.float32)
    projected = projected.reshape(pages_here, seq_len, 3, local_width)
    bias_full = jnp.stack([qv_bias[0], jnp.zeros_like(qv_bias[0]), qv_bias[1]]).astype(jnp.float32)
    projected = (projected + bias_full).astype(jnp.bfloat16)
    split_heads = projected.reshape(pages_here, seq_len, 3, heads_here, head_size)
    queries = split_heads[:, :, 0]
    keys_all = split_heads[:, :, 1]
    values_all = split_heads[:, :, 2]
    attended, log_total, bias_kept = lax.map(
        lambda single: page_forward(*single, table_all),
        (queries, keys_all, values_all, token_mask, ids_all),
    )
    attended_flat = attended.reshape(pages_here, seq_len, local_width)
    partial_out = jnp.dot(attended_flat, out_weight, preferred_element_type=jnp.float32)
    branch = lax.psum_scatter(
        partial_out.astype(jnp.bfloat16), "heads", scatter_dimension=1, tiled=True
    ).astype(jnp.float32) + out_bias.astype(jnp.float32)
    gain_one = first_gain.astype(jnp.float32)
    shift_one = first_shift.astype(jnp.float32)
    gain_two = second_gain.astype(jnp.float32)
    shift_two = second_shift.astype(jnp.float32)
    residual_one = hidden.astype(jnp.float32) + branch
    first_norm = layer_norm(residual_one, gain_one, shift_one)
    first_low = first_norm.astype(jnp.bfloat16)
    up_full, down_full, up_bias_full = (up_weight, down_weight, up_bias)
    ffn_input = lax.all_gather(first_low, "heads", axis=1, tiled=True)
    pre_act = jnp.dot(ffn_input, up_full, preferred_element_type=jnp.float32) + up_bias_full.astype(
        jnp.float32
    )
    activated = jax.nn.gelu(pre_act, approximate=False).astype(jnp.bfloat16)
    down_term = jnp.dot(activated, down_full, preferred_element_type=jnp.float32)
    ffn_out = lax.psum_scatter(
        down_term.astype(jnp.bfloat16), "heads", scatter_dimension=1, tiled=True
    ).astype(jnp.float32)
    second_sum = first_norm + ffn_out + down_bias.astype(jnp.float32)
    output = layer_norm(second_sum, gain_two, shift_two).astype(jnp.bfloat16)
    unused_two, second_pull = jax.vjp(layer_norm, second_sum, gain_two, shift_two)
    grad_second, grad_second_gain, grad_second_shift = second_pull(cotangent.astype(jnp.float32))
    grad_ffn = grad_second.astype(jnp.bfloat16)
    grad_down_bias = jnp.sum(grad_ffn, axis=(0, 1), dtype=jnp.float32)
    grad_ffn_all = lax.all_gather(grad_ffn, "heads", axis=1, tiled=True)
    grad_down = jnp.einsum(
        "psf,psd->fd", activated, grad_ffn_all, preferred_element_type=jnp.float32
    )
    grad_act = jnp.einsum(
        "psd,fd->psf", grad_ffn_all, down_full, preferred_element_type=jnp.float32
    )
    unused_gelu, gelu_pull = jax.vjp(partial(jax.nn.gelu, approximate=False), pre_act)
    grad_pre = gelu_pull(grad_act)[0].astype(jnp.bfloat16)
    grad_up = jnp.einsum("psd,psf->df", ffn_input, grad_pre, preferred_element_type=jnp.float32)
    grad_up_bias = jnp.sum(grad_pre, axis=(0, 1), dtype=jnp.float32)
    back_term = jnp.einsum("psf,df->psd", grad_pre, up_full, preferred_element_type=jnp.float32)
    grad_first_part = lax.psum_scatter(
        back_term.astype(jnp.bfloat16), "heads", scatter_dimension=1, tiled=True
    ).astype(jnp.float32)
    grad_first = grad_second + grad_first_part
    unused_one, first_pull = jax.vjp(layer_norm, residual_one, gain_one, shift_one)
    grad_residual, grad_first_gain, grad_first_shift = first_pull(grad_first)
    grad_branch = grad_residual.astype(jnp.bfloat16)
    grad_out_bias = jnp.sum(grad_branch, axis=(0, 1), dtype=jnp.float32)
    grad_branch_all = lax.all_gather(grad_branch, "heads", axis=1, tiled=True)
    grad_out_weight = jnp.einsum(
        "psc,psd->cd", attended_flat, grad_branch_all, preferred_element_type=jnp.float32
    )
    grad_attended = jnp.einsum(
        "psd,cd->psc", grad_branch_all, out_weight, preferred_element_type=jnp.float32
    )
    grad_att_heads = grad_attended.astype(jnp.bfloat16).reshape(
        pages_here, seq_len, heads_here, head_size
    )
    grad_queries, grad_keys, grad_values, grad_tables = lax.map(
        lambda single: page_backward(*single, table_all),
        (queries, keys_all, values_all, token_mask, ids_all, log_total, bias_kept, grad_att_heads),
    )
    tables_sum = jnp.sum(grad_tables, axis=0)
    grad_projected = jnp.stack([grad_queries, grad_keys, grad_values], axis=2).astype(jnp.bfloat16)
    grad_projected = grad_projected.reshape(pages_here, seq_len, 3 * local_width)
    grad_qkv = jnp.einsum(
        "psd,psc->dc", gathered, grad_projected, preferred_element_type=jnp.float32
    )
    grad_qkv = grad_qkv.reshape(model_width, 3, local_width)
    slice_sums = jnp.sum(grad_projected, axis=(0, 1), dtype=jnp.float32).reshape(3, local_width)
    grad_qv = jnp.stack([slice_sums[0], slice_sums[2]])
    input_term = jnp.einsum(
        "psc,dc->psd", grad_projected, weight_flat, preferred_element_type=jnp.float32
    )
    grad_input = grad_residual + lax.psum_scatter(
        input_term.astype(jnp.bfloat16), "heads", scatter_dimension=1, tiled=True
    ).astype(jnp.float32)
    grad_relative = tables_sum[:rel_count]
    grad_horizontal = tables_sum[rel_count : rel_count + pos_count]
    grad_vertical = tables_sum[rel_count + pos_count :]
    (
        grad_qkv,
        grad_qv,
        grad_out_weight,
        grad_up,
        grad_up_bias,
        grad_down,
        grad_relative,
        grad_horizontal,
        grad_vertical,
    ) = lax.psum(
        (
            grad_qkv,
            grad_qv,
            grad_out_weight,
            grad_up,
            grad_up_bias,
            grad_down,
            grad_relative,
            grad_horizontal,
            grad_vertical,
        ),
        "pages",
    )
    (
        grad_first_gain,
        grad_first_shift,
        grad_second_gain,
        grad_second_shift,
        grad_out_bias,
        grad_down_bias,
    ) = lax.psum(
        (
            grad_first_gain,
            grad_first_shift,
            grad_second_gain,
            grad_second_shift,
            grad_out_bias,
            grad_down_bias,
        ),
        ("pages", "heads"),
    )
    return (
        output,
        grad_input.astype(jnp.bfloat16),
        grad_qkv,
        grad_qv,
        grad_out_weight,
        grad_out_bias,
        grad_first_gain,
        grad_first_shift,
        grad_up,
        grad_up_bias,
        grad_down,
        grad_down_bias,
        grad_second_gain,
        grad_second_shift,
        grad_relative,
        grad_horizontal,
        grad_vertical,
    )


def solution(mesh):
    in_specs = (
        P("pages", "heads", None),
        P(None, None, "heads"),
        P(None, "heads"),
        P("heads", None),
        P(),
        P(),
        P(),
        P(None, "heads"),
        P("heads"),
        P("heads", None),
        P(),
        P(),
        P(),
        P(None, "heads"),
        P(None, "heads"),
        P(None, "heads"),
        P("pages", None),
        P("pages", None, None),
        P("pages", None, None),
        P("pages", None, None),
        P("pages", "heads", None),
    )
    out_specs = (
        P("pages", "heads", None),
        P("pages", "heads", None),
        P(None, None, "heads"),
        P(None, "heads"),
        P("heads", None),
        P(),
        P(),
        P(),
        P(None, "heads"),
        P("heads"),
        P("heads", None),
        P(),
        P(),
        P(),
        P(None, "heads"),
        P(None, "heads"),
        P(None, "heads"),
    )
    return jax.shard_map(shards, mesh=mesh, in_specs=in_specs, out_specs=out_specs, check_vma=False)
```

profile of v0, /device:TPU:0, one launch (start us, length us, event | category | flops | bytes accessed | tf_op | source)
XLA Modules:
  0.0 1130.4 jit_solution(14571961566761630700)
XLA Ops:
  17.6 36.6 %all-gather.5.cloned.1.call-done = bf16[2,608,768]{2,1,0:T(8,128)(2,1)} async-done(((bf16[2,152,768]{2,1,0:T(8,128)(2,1)}), bf16[2,608,768]{2,1,0:T(8,128)(2,1)}) %all-gather.5.cloned.1.call-update) | async-done | bytes 1867792 | tf_op jit(solution)/shard_map/all_gather | solution.py:144
  57.3 289.6 %while.52 = (s32[]{:T(128)}, bf16[2,608,3,64]{1,3,2,0:T(8,128)(2,1)}, f32[2,3,608,1]{2,1,3,0:T(4,128)S(1)}, f32[2,3,608,608]{3,2,1,0:T(8,128)}, bf16[2,608,3,64]...) while((s32[]{:T(128)}, ...), condition=%wide.region_5.6_spmd, body=%wide.region_0.5_spmd.sunk | while | flops 374215488 | bytes 101524744 | solution.py:154
  62.3 6.7 reshape.265
  69.0 100.8 %while.55 = (s32[]{:T(128)}, f32[8,3,46208]{2,1,0:T(4,128)}, s32[8,3,46208]{2,0,1:T(8,128)}, bf16[3,160]{1,0:T(4,128)(2,1)S(1)}, s32[]{:T(128)}, /*index=5*/s32[]{:T(128)}, s32[]{}, s32[]{}) while((s32[]{:T(128)}, f32[8,3,46208]{2,1,0:T(4,128)}, s32[8,3,46208]{2,0,1:T(8,128)}, bf16[3,160]{1,0:T(4,128)(2,1)S(1)}, s32[]{:T(128)}, ...), condition=%wide.region_2.2_spmd, body=%wide.region_1.1_spmd.sunk | while | flops 81326080 | bytes 2403909 | solution.py:43
  72.7 8.9 fusion.176
  85.3 8.9 fusion.176
  97.9 8.9 fusion.176
  110.5 8.9 fusion.176
  123.1 8.9 fusion.176
  135.7 8.9 fusion.176
  148.3 8.9 fusion.176
  160.9 8.8 fusion.176
  174.8 6.5 broadcast_in_dim.126
  181.4 6.5 reshape.266
  187.9 6.1 copy.136
  206.9 6.7 reshape.265
  213.6 100.8 %while.55 = (s32[]{:T(128)}, f32[8,3,46208]{2,1,0:T(4,128)}, s32[8,3,46208]{2,0,1:T(8,128)}, bf16[3,160]{1,0:T(4,128)(2,1)S(1)}, s32[]{:T(128)}, /*index=5*/s32[]{:T(128)}, s32[]{}, s32[]{}) while((s32[]{:T(128)}, f32[8,3,46208]{2,1,0:T(4,128)}, s32[8,3,46208]{2,0,1:T(8,128)}, bf16[3,160]{1,0:T(4,128)(2,1)S(1)}, s32[]{:T(128)}, ...), condition=%wide.region_2.2_spmd, body=%wide.region_1.1_spmd.sunk | while | flops 81326080 | bytes 2403909 | solution.py:43
  217.4 8.9 fusion.176
  230.0 8.9 fusion.176
  242.6 8.9 fusion.176
  255.2 8.9 fusion.176
  267.8 8.9 fusion.176
  280.4 8.9 fusion.176
  293.0 8.9 fusion.176
  305.6 8.8 fusion.176
  319.5 6.5 broadcast_in_dim.126
  326.0 6.5 reshape.266
  332.5 6.1 copy.136
  352.5 38.9 %reduce-scatter.13.cloned.1.call-done = bf16[152,1536]{1,0:T(8,128)(2,1)} async-done(((bf16[608,1536]{1,0:T(8,128)(2,1)}), bf16[152,1536]{1,0:T(8,128)(2,1)}) %reduce-scatter.13.cloned.1.call-update) | async-done | bytes 466960
  394.1 41.0 %all-gather.7.cloned.1.call-done = bf16[2,608,768]{2,1,0:T(8,128)(2,1)} async-done(((bf16[2,152,768]{2,1,0:T(8,128)(2,1)}), bf16[2,608,768]{2,1,0:T(8,128)(2,1)}) %all-gather.7.cloned.1.call-update) | async-done | bytes 1867792 | tf_op jit(solution)/shard_map/all_gather | solution.py:171
  439.3 9.6 multiply_convert_fusion.1
  455.9 38.4 %reduce-scatter.15.cloned.1.call-done = bf16[152,1536]{1,0:T(8,128)(2,1)} async-done(((bf16[608,1536]{1,0:T(8,128)(2,1)}), bf16[152,1536]{1,0:T(8,128)(2,1)}) %reduce-scatter.15.cloned.1.call-update) | async-done | bytes 466960
  503.0 41.0 %all-gather.9.cloned.1.call-done = bf16[2,608,768]{2,1,0:T(8,128)(2,1)} async-done(((bf16[2,152,768]{2,1,0:T(8,128)(2,1)}), bf16[2,608,768]{2,1,0:T(8,128)(2,1)}) %all-gather.9.cloned.1.call-update) | async-done | bytes 1867792 | tf_op jit(solution)/shard_map/all_gather | solution.py:186
  544.0 7.3 convert_reduce_fusion
  557.9 38.9 %reduce-scatter.17.cloned.1.call-done = bf16[152,1536]{1,0:T(8,128)(2,1)} async-done(((bf16[608,1536]{1,0:T(8,128)(2,1)}), bf16[152,1536]{1,0:T(8,128)(2,1)}) %reduce-scatter.17.cloned.1.call-update) | async-done | bytes 466960
  605.2 41.0 %all-gather.11.cloned.1.call-done = bf16[2,608,768]{2,1,0:T(8,128)(2,1)} async-done(((bf16[2,152,768]{2,1,0:T(8,128)(2,1)}), bf16[2,608,768]{2,1,0:T(8,128)(2,1)}) %all-gather.11.cloned.1.call-update) | async-done | bytes 1867792 | tf_op jit(solution)/shard_map/all_gather | solution.py:206
  649.2 302.5 %while.54 = (s32[]{:T(128)}, bf16[2,608,3,64]{1,3,2,0:T(8,128)(2,1)}, bf16[2,608,3,64]{1,3,2,0:T(8,128)(2,1)}, bf16[2,608,3,64]{1,3,2,0:T(8,128)(2,1)}, f32[2,16...) while((s32[]{:T(128)}, ...), condition=%wide.region_21.22_spmd, body=%wide.region_17.21_spmd.sunk | while | flops 802404096 | bytes 122301768 | solution.py:216
  658.5 6.7 reshape.267
  670.1 6.1 copy.137
  676.2 5.6 multiply_reduce_fusion.6
  700.4 99.9 %while.56 = (s32[]{:T(128)}, f32[160,3]{0,1:T(4,128)S(1)}, s32[8,3,46208]{2,0,1:T(8,128)}, bf16[8,3,46208]{2,1,0:T(4,128)(2,1)}, s32[]{:T(128)}, /*index=5*/s32[]{:T(128)}, s32[]{}, s32[]{}) while((s32[]{:T(128)}, f32[160,3]{0,1:T(4,128)S(1)}, s32[8,3,46208]{2,0,1:T(8,128)}, bf16[8,3,46208]{2,1,0:T(4,128)(2,1)}, s32[]{:T(128)}, ...), condition=%wide.region_20.20_spmd.clone, body=%wide.region_19.19_spmd.clone.sunk | while | flops 81327040 | bytes 2037135 | solution.py:59
  704.3 8.7 fusion.172
  716.7 8.7 fusion.172
  729.2 8.7 fusion.172
  741.7 8.7 fusion.172
  754.2 8.7 fusion.172
  766.7 8.7 fusion.172
  779.2 8.7 fusion.172
  791.7 8.7 fusion.172
  809.6 6.7 reshape.267
  821.1 6.1 copy.137
  827.3 5.6 multiply_reduce_fusion.6
  851.5 99.9 %while.56 = (s32[]{:T(128)}, f32[160,3]{0,1:T(4,128)S(1)}, s32[8,3,46208]{2,0,1:T(8,128)}, bf16[8,3,46208]{2,1,0:T(4,128)(2,1)}, s32[]{:T(128)}, /*index=5*/s32[]{:T(128)}, s32[]{}, s32[]{}) while((s32[]{:T(128)}, f32[160,3]{0,1:T(4,128)S(1)}, s32[8,3,46208]{2,0,1:T(8,128)}, bf16[8,3,46208]{2,1,0:T(4,128)(2,1)}, s32[]{:T(128)}, ...), condition=%wide.region_20.20_spmd.clone, body=%wide.region_19.19_spmd.clone.sunk | while | flops 81327040 | bytes 2037135 | solution.py:59
  855.3 8.7 fusion.172
  867.8 8.7 fusion.172
  880.3 8.7 fusion.172
  892.8 8.7 fusion.172
  905.3 8.7 fusion.172
  917.8 8.7 fusion.172
  930.2 8.7 fusion.172
  942.7 8.7 fusion.172
  973.2 40.8 %all-reduce = (f32[768]{0:T(1024)}, f32[768]{0:T(1024)}, f32[768]{0:T(1024)}, f32[768]{0:T(1024)}, f32[768]{0:T(1024)}, /*index=5*/f32[768]{0:T(1024)}) all-reduce(f32[768]{0:T(1024)S(1)} %copy-done.37, f32[768]{0:T(1024)S(1)} %copy-done.35, f32[768]{0:T(1024)S(1)} %copy-done.36, ...), channel_id=1, replica_groups=mesh['pages'=8,'heads'=4] {'pages','heads'}, use_global_device_ids=true, to_apply=%region_28.29 | all-reduce | flops 4608 | bytes 36864 | tf_op jit(solution)/shard_map/psum | solution.py:269
  1014.2 25.1 %all-reduce.1 = (f32[2,192]{1,0:T(2,128)}, f32[768]{0:T(1024)}, f32[32,3]{0,1:T(4,128)}, f32[64,3]{0,1:T(4,128)}, f32[64,3]{0,1:T(4,128)}) all-reduce(f32[2,192]{1,0:T(2,128)S(1)} %pad_maximum_fusion, f32[768]{0:T(1024)S(1)} %copy-done.38, f32[32,3]{0,1:T(4,128)S(1)} %slice.82, ...), channel_id=1, replica_groups=mesh['pages'=8,'heads'=4] {'pages'}, use_global_device_ids=true, to_apply=%region_25.26 | all-reduce | flops 1632 | bytes 13056 | tf_op jit(solution)/shard_map/psum | solution.py:248
  1041.4 75.6 %all-reduce.5.cloned.1.call-done = (f32[768,3,192]{0,2,1:T(8,128)}, f32[192,768]{1,0:T(8,128)}, f32[768,768]{1,0:T(8,128)}, f32[768,768]{1,0:T(8,128)}) async-done(((f32[768,3,192]{0,2,1:T(8,128)}, f32[192,768]{1,0:T(8,128)}, f32[768,768]{1,0:T(8,128)}, f32[768,768]{1,0:T(8,128)}), (f32[768,3,192]{0,2,1:T(8,128)}, f32[192,768]{1,0:T(8,128)}, f32[768,768]{1,0:T(8,128)}, ...) | async-done | bytes 7077904 | tf_op jit(solution)/shard_map/psum | solution.py:248
  (312 shorter events, 311.1 us)
Async XLA Ops:
  7.2 428.0 %copy-start = (bf16[768,768]{1,0:T(8,128)(2,1)S(1)}, bf16[768,768]{1,0:T(8,128)(2,1)}, u32[]{:S(2)}) copy-start(bf16[768,768]{1,0:T(8,128)(2,1)} %param.36) | copy-start | bytes 3538948
  7.2 47.0 %all-gather.5.cloned.1.call-start = ((), (), s32[]{:S(2)}) async-start(), calls=%async_computation.4 | async-start | bytes 2334720 | tf_op jit(solution)/shard_map/all_gather | solution.py:144
  7.9 383.4 %reduce-scatter.13.cloned.1.call-start = ((), (), s32[]{:S(2)}) async-start(), calls=%async_computation.8 | async-start | bytes 2334720
  9.7 3.7 copy-start.16
  13.4 40.8 %copy-start.49 = (bf16[768,3,192]{0,2,1:T(8,128)(2,1)S(1)}, bf16[768,3,192]{0,2,1:T(8,128)(2,1)}, u32[]{:S(2)}) copy-start(bf16[768,3,192]{0,2,1:T(8,128)(2,1)} %param.30) | copy-start | bytes 2654212
  17.6 39.6 %copy-start.29 = (s32[2,608]{1,0:T(2,128)S(1)}, s32[2,608]{1,0:T(2,128)}, u32[]{:S(2)}) copy-start(s32[2,608]{1,0:T(2,128)} %param.45) | copy-start | bytes 14596
  57.2 289.6 %copy-start.28 = (bf16[192,768]{1,0:T(8,128)(2,1)S(1)}, bf16[192,768]{1,0:T(8,128)(2,1)}, u32[]{:S(2)}) copy-start(bf16[192,768]{1,0:T(8,128)(2,1)} %param.32) | copy-start | bytes 884740
  193.9 5.6 slice-start.2
  197.6 1.9 slice-start.3
  199.6 2.5 copy-start.20
  338.6 5.6 slice-start.2
  342.3 1.9 slice-start.3
  344.2 2.4 copy-start.20
  346.9 5.5 copy-start.10
  350.7 1.7 copy-start.39
  350.8 1.7 copy-start.40
  350.8 1.7 copy-start.41
  350.8 41.7 %copy-start.9 = (bf16[2,152,768]{2,1,0:T(8,128)(2,1)S(1)}, bf16[2,152,768]{2,1,0:T(8,128)(2,1)}, u32[]{:S(2)}) copy-start(bf16[2,152,768]{2,1,0:T(8,128)(2,1)} %param.29) | copy-start | bytes 1400836
  352.3 41.8 %copy-start.42 = (bf16[768]{0:T(1024)(128)(2,1)S(1)}, bf16[768]{0:T(1024)(128)(2,1)}, u32[]{:S(2)}) copy-start(bf16[768]{0:T(1024)(128)(2,1)} %param.37) | copy-start | bytes 4612
  352.4 82.8 %all-gather.7.cloned.1.call-start = ((), (), s32[]{:S(2)}) async-start(), calls=%async_computation.5 | async-start | bytes 2334720 | tf_op jit(solution)/shard_map/all_gather | solution.py:171
  394.1 100.2 %reduce-scatter.15.cloned.1.call-start = ((), (), s32[]{:S(2)}) async-start(), calls=%async_computation.9 | async-start | bytes 2334720
  439.3 9.6 copy-start.15
  439.3 10.8 copy-start.48
  453.7 2.1 copy-start.43
  453.7 2.1 copy-start.44
  455.3 88.7 %all-gather.9.cloned.1.call-start = ((), (), s32[]{:S(2)}) async-start(), calls=%async_computation.6 | async-start | bytes 2334720 | tf_op jit(solution)/shard_map/all_gather | solution.py:186
  496.2 3.9 copy-start.14
  497.7 3.5 copy-start.7
  502.9 93.9 %reduce-scatter.17.cloned.1.call-start = ((), (), s32[]{:S(2)}) async-start(), calls=%async_computation.10 | async-start | bytes 2334720
  556.2 42.5 %copy-start.8 = (f32[2,152,768]{2,1,0:T(8,128)S(1)}, f32[2,152,768]{2,1,0:T(8,128)}, u32[]{:S(2)}) copy-start(f32[2,152,768]{2,1,0:T(8,128)} %copy-done.7) | copy-start | bytes 2801668
  557.8 88.4 %all-gather.11.cloned.1.call-start = ((), (), s32[]{:S(2)}) async-start(), calls=%async_computation.7 | async-start | bytes 2334720 | tf_op jit(solution)/shard_map/all_gather | solution.py:206
  602.1 47.1 %copy-start.11 = (bf16[2,608,3,64]{1,3,2,0:T(8,128)(2,1)S(1)}, bf16[2,608,3,64]{1,3,2,0:T(8,128)(2,1)}, u32[]{:S(2)}) copy-start(bf16[2,608,3,64]{1,3,2,0:T(8,128)(2,1)} %copy-done.10) | copy-start | bytes 1400836
  602.6 46.6 %copy-start.30 = (f32[2,152]{1,0:T(2,128)}, f32[2,152]{1,0:T(2,128)S(1)}, u32[]{:S(2)}) copy-start(f32[2,152]{1,0:T(2,128)S(1)} %negate_multiply_fusion.1) | copy-start | bytes 3652
  605.1 434.2 %reduce-scatter.19.cloned.1.call-start = ((), (), s32[]{:S(2)}) async-start(), calls=%async_computation.11 | async-start | bytes 2334720
  649.4 36.1 %copy-start.5 = (bf16[2,608,3,64]{1,3,2,0:T(8,128)(2,1)}, bf16[2,608,3,64]{1,3,2,0:T(8,128)(2,1)S(1)}, u32[]{:S(2)}) copy-start(bf16[2,608,3,64]{1,3,2,0:T(8,128)(2,1)S(1)} %get-tuple-element.768) | copy-start | bytes 1400836 | tf_op jit(solution)/shard_map/while
  649.4 37.6 %copy-start.3 = (bf16[2,608,3,64]{1,3,2,0:T(8,128)(2,1)}, bf16[2,608,3,64]{1,3,2,0:T(8,128)(2,1)S(1)}, u32[]{:S(2)}) copy-start(bf16[2,608,3,64]{1,3,2,0:T(8,128)(2,1)S(1)} %get-tuple-element.766) | copy-start | bytes 1400836 | tf_op jit(solution)/shard_map/while
  670.1 11.7 %slice-start = ((s8[4669440]{0:T(1024)(128)(4,1)}), s8[475136]{0:T(1024)(128)(4,1)S(1)}, s32[]{:S(2)}) async-start(s8[4669440]{0:T(1024)(128)(4,1)} %bitcast.280), calls=%async_computation.13 | async-start | bytes 950272 | tf_op jit(solution)/shard_map/while
  676.2 5.6 slice-start.1
  682.7 4.3 copy-start.2
  700.4 100.0 %copy-start.4 = (bf16[2,608,3,64]{1,3,2,0:T(8,128)(2,1)S(1)}, bf16[2,608,3,64]{1,3,2,0:T(8,128)(2,1)}, u32[]{:S(2)}) copy-start(bf16[2,608,3,64]{1,3,2,0:T(8,128)(2,1)} %copy-done.3) | copy-start | bytes 1400836 | tf_op jit(solution)/shard_map/while
  700.4 100.0 %copy-start.6 = (bf16[2,608,3,64]{1,3,2,0:T(8,128)(2,1)S(1)}, bf16[2,608,3,64]{1,3,2,0:T(8,128)(2,1)}, u32[]{:S(2)}) copy-start(bf16[2,608,3,64]{1,3,2,0:T(8,128)(2,1)} %copy-done.5) | copy-start | bytes 1400836 | tf_op jit(solution)/shard_map/while
  800.4 36.1 %copy-start.5 = (bf16[2,608,3,64]{1,3,2,0:T(8,128)(2,1)}, bf16[2,608,3,64]{1,3,2,0:T(8,128)(2,1)S(1)}, u32[]{:S(2)}) copy-start(bf16[2,608,3,64]{1,3,2,0:T(8,128)(2,1)S(1)} %get-tuple-element.768) | copy-start | bytes 1400836 | tf_op jit(solution)/shard_map/while
  800.5 37.6 %copy-start.3 = (bf16[2,608,3,64]{1,3,2,0:T(8,128)(2,1)}, bf16[2,608,3,64]{1,3,2,0:T(8,128)(2,1)S(1)}, u32[]{:S(2)}) copy-start(bf16[2,608,3,64]{1,3,2,0:T(8,128)(2,1)S(1)} %get-tuple-element.766) | copy-start | bytes 1400836 | tf_op jit(solution)/shard_map/while
  821.1 11.7 %slice-start = ((s8[4669440]{0:T(1024)(128)(4,1)}), s8[475136]{0:T(1024)(128)(4,1)S(1)}, s32[]{:S(2)}) async-start(s8[4669440]{0:T(1024)(128)(4,1)} %bitcast.280), calls=%async_computation.13 | async-start | bytes 950272 | tf_op jit(solution)/shard_map/while
  827.3 5.6 slice-start.1
  833.8 4.3 copy-start.2
  851.5 100.0 %copy-start.4 = (bf16[2,608,3,64]{1,3,2,0:T(8,128)(2,1)S(1)}, bf16[2,608,3,64]{1,3,2,0:T(8,128)(2,1)}, u32[]{:S(2)}) copy-start(bf16[2,608,3,64]{1,3,2,0:T(8,128)(2,1)} %copy-done.3) | copy-start | bytes 1400836 | tf_op jit(solution)/shard_map/while
  851.5 100.0 %copy-start.6 = (bf16[2,608,3,64]{1,3,2,0:T(8,128)(2,1)S(1)}, bf16[2,608,3,64]{1,3,2,0:T(8,128)(2,1)}, u32[]{:S(2)}) copy-start(bf16[2,608,3,64]{1,3,2,0:T(8,128)(2,1)} %copy-done.5) | copy-start | bytes 1400836 | tf_op jit(solution)/shard_map/while
  951.7 3.0 copy-start.50
  958.3 2.1 copy-start.23
  960.0 157.1 %all-reduce.5.cloned.1.call-start = ((), (), s32[]{:S(2)}) async-start(), calls=%async_computation.12 | async-start | bytes 14155776 | tf_op jit(solution)/shard_map/psum | solution.py:248
  960.4 4.8 copy-start.47
  960.4 4.8 copy-start.52
  965.2 3.2 copy-start.21
  965.2 3.2 copy-start.24
  965.2 4.6 copy-start.26
  965.2 4.6 copy-start.46
  972.4 41.8 %copy-start.38 = (f32[768]{0:T(1024)S(1)}, f32[768]{0:T(1024)}, u32[]{:S(2)}) copy-start(f32[768]{0:T(1024)} %get-tuple-element.387) | copy-start | bytes 9220
  972.4 68.0 %copy-start.13 = (f32[2,152,768]{2,1,0:T(8,128)S(1)}, f32[2,152,768]{2,1,0:T(8,128)}, u32[]{:S(2)}) copy-start(f32[2,152,768]{2,1,0:T(8,128)} %copy-done.12) | copy-start | bytes 2801668
  972.5 68.0 %copy-start.31 = (f32[2,152]{1,0:T(2,128)S(1)}, f32[2,152]{1,0:T(2,128)}, u32[]{:S(2)}) copy-start(f32[2,152]{1,0:T(2,128)} %copy-done.30) | copy-start | bytes 3652
  1117.0 3.0 copy-start.27
  1117.0 3.8 copy-start.18
  1120.0 2.2 copy-start.17
  1120.0 3.6 copy-start.1
  (13 other events, 12.6 us)
Sparse Core Ops, SparseCore 0:
  9.6 44.5 all-gather.4
  352.5 38.8 reduce-scatter.12
  394.2 40.9 all-gather.6
  455.4 38.8 reduce-scatter.14
  503.1 40.9 all-gather.8
  557.9 38.8 reduce-scatter.16
  605.2 40.9 all-gather.10
  960.1 39.5 reduce-scatter.18
  1004.5 112.4 all-reduce.4
where the time goes:
time: 1140 us; the launch traced here: 1130 us
  matrix products  357 us (31%)
  waiting for transfers between devices  352 us (31%)
  local copies, waits for them, and re-layouts  301 us (26%)
  blocking collectives  65.9 us (6%)
  other arithmetic  37.6 us (3%)
  between operations  14.7 us (1%)
    dot_general x16, matrix products, one_part(): jnp.dot(table_all, bucket_onehot(ids_piece, buckets), preferred_element_t...  142 us
    dot_general x16, matrix products, add_part(): lax.dot_general(onehot, grad_piece, (((1,), (1,)), ((), ())), preferred_e...  139 us
    slice x32, local copies, waits for them, and re-layouts, bucket_onehot(): ids_piece[0][None, :] == levels  121 us
    unnamed x13, waiting for transfers between devices  117 us
    psum x1, waiting for transfers between devices, shards(): lax.psum((grad_qkv, grad_qv, grad_out_weight, grad_up, grad_up_bias, grad...  75.6 us
    all_gather x1, waiting for transfers between devices, shards(): grad_ffn_all = lax.all_gather(grad_ffn, 'heads', axis=1, tiled=True)  41 us
    all_gather x1, waiting for transfers between devices, shards(): ffn_input = lax.all_gather(first_low, 'heads', axis=1, tiled=True)  41 us
    all_gather x1, waiting for transfers between devices, shards(): grad_branch_all = lax.all_gather(grad_branch, 'heads', axis=1, tiled=True)  41 us
  transfers between devices with their start and end apart: 9, of which 8 were waited for; matrix products, arithmetic and copies ran while one was open for 2% of the time, Pallas kernels for 0%

commit v1 on v0

v1 whole, which is shorter than its diff:
```python
import jax
import jax.numpy as jnp
from jax import lax
from jax.experimental import pallas as pl
from jax.experimental.pallas import tpu as pltpu
from jax.sharding import PartitionSpec as P
bf=jnp.bfloat16; f32=jnp.float32

def nn(a,b): return lax.dot_general(a,b,(((1,),(0,)),((),())),preferred_element_type=f32)
def nt(a,b): return lax.dot_general(a,b,(((1,),(1,)),((),())),preferred_element_type=f32)
def tn(a,b): return lax.dot_general(a,b,(((0,),(0,)),((),())),preferred_element_type=f32)

def ln_stats(v):
    mu=jnp.mean(v,axis=-1,keepdims=True)
    c=v-mu
    r=lax.rsqrt(jnp.mean(c*c,axis=-1,keepdims=True)+1e-12)
    return c*r,r

class Cfg: pass

def compute_kernel(c, koff_fn, xf, ct, i1, i2, i3, mask, wa, wu, wd, qvb, ub, tab, vec,
                   out_o, dh_o, ga_h, gu_h, gd_h, sm_o, tg_o,
                   wav, wuv, wdv, wsem, gsem, bias, PR, QT, KT, VT, att, fn, n1, r1s, act, gp, dsb, dOT, acc, dQ, dKV, flow, dffn, dsec):
    R=c.R; S=c.S; Z=c.Z; H=c.H; HD=c.HD; D=c.D; SP=c.SP; L=H*HD
    koff=koff_fn()
    cps=[pltpu.make_async_copy(a,b,wsem.at[j]) for j,(a,b) in enumerate(((wa,wav),(wu,wuv),(wd,wdv)))]
    for cp in cps: cp.start()
    wa,wu,wd=wav,wuv,wdv
    gcp=[]
    ga_o,gu_o,gd_o=wa,wu,wd
    own=lambda: xf[pl.ds(koff,R),:]
    nl=SP//128
    def bias_body(q,_):
        i=pl.multiple_of(q*8,8)
        for l in range(nl):
            w=min(128,S-l*128)
            sl=pl.ds(l*128,w)
            idx=[]
            for r in (i1,i2,i3):
                v=r[pl.ds(i,8),sl]
                if w<128: v=jnp.concatenate([v,jnp.zeros((8,128-w),jnp.int32)],axis=1)
                idx.append(v)
            for h in range(Z*H):
                g=None
                for t in range(3):
                    row=jnp.broadcast_to(tab[t,h:h+1,:],(8,128))
                    x=jnp.take_along_axis(row,idx[t],axis=1,mode="promise_in_bounds")
                    g=x if g is None else g+x
                bias[h,pl.ds(i,8),pl.ds(l*128,128)]=g
        return 0
    lax.fori_loop(0,R//8,bias_body,0)
    cps[0].wait()
    def qkv_body(z,_):
        bcol=jnp.transpose(qvb[z])
        q=nt(wa[z,0:L,:],own())+bcol[0:L,0:1]
        QT[z]=q.astype(bf)*jnp.bfloat16(0.125)
        KT[z]=nt(wa[z,L:2*L,:],xf[...]).astype(bf)
        VT[z]=(nt(wa[z,2*L:3*L,:],xf[...])+bcol[L:2*L,0:1]).astype(bf)
        return 0
    lax.fori_loop(0,Z,qkv_body,0)
    CH=16
    def fwd_body(z,_):
        outs=[]
        for hl in range(H):
            h=z*H+hl
            rs=slice(hl*HD,(hl+1)*HD)
            bias[h]=bias[h]+tn(QT[z,rs,:],KT[z,rs,:])
            def chunk(q,_):
                i=pl.multiple_of(q*CH,CH)
                s=bias[h,pl.ds(i,CH),:]
                s=jnp.where(mask[0:1,:]>0,s,-1e9)
                m=jnp.max(s,axis=-1,keepdims=True)
                e=jnp.exp(s-m)
                p=e*(1.0/jnp.sum(e,axis=-1,keepdims=True))
                PR[h,pl.ds(i,CH),:]=p.astype(bf)
                return 0
            lax.fori_loop(0,R//CH,chunk,0,unroll=True)
            outs.append(nt(PR[h],VT[z,rs,:]).astype(bf))
        att[z]=jnp.concatenate(outs,axis=1)
        return 0
    lax.fori_loop(0,Z,fwd_body,0)
    acc[...]=own().astype(f32)+vec[0:1,:]
    def out_body(z,_):
        acc[...]+=nn(att[z],wa[z,3*L:4*L,:])
        return 0
    lax.fori_loop(0,Z,out_body,0)
    def ln1(q,_):
        i=pl.multiple_of(q*CH,CH); s=pl.ds(i,CH)
        n,r=ln_stats(acc[s,:])
        n1[s,:]=n; r1s[s,:]=jnp.broadcast_to(r,(CH,128))
        f=n*vec[1:2,:]+vec[2:3,:]
        fn[s,:]=f; flow[s,:]=f.astype(bf)
        return 0
    lax.fori_loop(0,R//CH,ln1,0,unroll=True)
    cps[1].wait(); cps[2].wait()
    acc[...]=fn[...]+vec[3:4,:]
    FZ=c.FZ
    def ffn_body(z,_):
        for n0 in range(0,FZ,256):
            ns=slice(n0,n0+256)
            pre=nn(flow[...],wu[z,:,ns])+ub[z,0:1,ns]
            phi=0.5*(1.0+lax.erf(pre*0.7071067811865476))
            act[z,:,ns]=(pre*phi).astype(bf)
            gp[z,:,ns]=(phi+pre*(0.3989422804014327*jnp.exp(-0.5*pre*pre))).astype(bf)
        acc[...]+=nn(act[z],wd[z])
        return 0
    lax.fori_loop(0,Z,ffn_body,0)
    zero=jnp.zeros((8,D),f32)
    def rsum(x): return jnp.sum(x.reshape(x.shape[0]//8,8,D),axis=0)
    def ln2(q,car):
        a,b,d=car
        i=pl.multiple_of(q*CH,CH); s=pl.ds(i,CH)
        n,r=ln_stats(acc[s,:])
        out_o[s,:]=(n*vec[4:5,:]+vec[5:6,:]).astype(bf)
        g=ct[s,:].astype(f32)
        gg=g*vec[4:5,:]
        ds=r*(gg-jnp.mean(gg,axis=-1,keepdims=True)-n*jnp.mean(gg*n,axis=-1,keepdims=True))
        dsec[s,:]=ds
        lo=ds.astype(bf); dffn[s,:]=lo
        return (a+rsum(g*n),b+rsum(g),d+rsum(lo.astype(f32)))
    a,b,d=lax.fori_loop(0,R//CH,ln2,(zero,zero,zero),unroll=True)
    sm_o[4:5,:]=jnp.sum(a,axis=0,keepdims=True); sm_o[5:6,:]=jnp.sum(b,axis=0,keepdims=True); sm_o[3:4,:]=jnp.sum(d,axis=0,keepdims=True)
    def ffb_body(z,_):
        dp=(nt(dffn[...],wd[z])*gp[z].astype(f32)).astype(bf)
        gd_o[z]=tn(act[z],dffn[...]).astype(bf)
        act[z]=dp
        sm_o[pl.ds(8+z*8,8),:]=nn(jnp.ones((8,R),bf),dp)
        dsec[...]+=nt(dp,wu[z])
        gu_o[z]=tn(flow[...],dp).astype(bf)
        return 0
    lax.fori_loop(0,Z,ffb_body,0)
    def ln1b(q,car):
        a,b,d=car
        i=pl.multiple_of(q*CH,CH); s=pl.ds(i,CH)
        n=n1[s,:]; r=r1s[s,0:1]; g=dsec[s,:]
        gg=g*vec[1:2,:]
        ds=r*(gg-jnp.mean(gg,axis=-1,keepdims=True)-n*jnp.mean(gg*n,axis=-1,keepdims=True))
        fn[s,:]=ds
        lo=ds.astype(bf); dffn[s,:]=lo
        return (a+rsum(g*n),b+rsum(g),d+rsum(lo.astype(f32)))
    a,b,d=lax.fori_loop(0,R//CH,ln1b,(zero,zero,zero),unroll=True)
    sm_o[1:2,:]=jnp.sum(a,axis=0,keepdims=True); sm_o[2:3,:]=jnp.sum(b,axis=0,keepdims=True); sm_o[0:1,:]=jnp.sum(d,axis=0,keepdims=True)
    dh_o[...]=jnp.zeros(dh_o.shape,f32)
    dh_o[pl.ds(koff,R),:]=fn[...]
    def bwd_body(z,_):
        dOT[...]=nt(wa[z,3*L:4*L,:],dffn[...]).astype(bf)
        ga_o[z,3*L:4*L,:]=tn(att[z],dffn[...]).astype(bf)
        for hl in range(H):
            h=z*H+hl
            rs=slice(hl*HD,(hl+1)*HD)
            bias[h]=tn(dOT[rs,:],VT[z,rs,:])
            def chunk(q,_):
                i=pl.multiple_of(q*CH,CH); s=pl.ds(i,CH)
                p=PR[h,s,:].astype(f32); dp=bias[h,s,:]
                inner=jnp.sum(p*dp,axis=-1,keepdims=True)
                ds=p*(dp-inner)
                bias[h,s,:]=ds
                dsb[s,:]=ds.astype(bf)
                return 0
            lax.fori_loop(0,R//CH,chunk,0,unroll=True)
            dQ[rs,:]=(nt(KT[z,rs,:],dsb[...])*0.125).astype(bf)
            dKV[hl*HD:(hl+1)*HD,:]=nn(QT[z,rs,:],dsb[...]).astype(bf)
            dKV[L+hl*HD:L+(hl+1)*HD,:]=nn(dOT[rs,:],PR[h]).astype(bf)
        sm_o[pl.ds(40+z*8,8),0:L]=nt(jnp.ones((8,R),bf),dQ[...])
        sm_o[pl.ds(72+z*8,8),0:L]=nt(jnp.ones((8,SP),bf),dKV[L:2*L,:])
        dh_o[pl.ds(koff,R),:]+=tn(dQ[...],wa[z,0:L,:])
        dh_o[...]+=tn(dKV[...],wa[z,L:3*L,:])
        ga_o[z,0:L,:]=nn(dQ[...],own()).astype(bf)
        ga_o[z,L:3*L,:]=nn(dKV[...],xf[...]).astype(bf)
        return 0
    lax.fori_loop(0,Z,bwd_body,0)
    for j,(a,b) in enumerate(((wa,ga_h),(wu,gu_h),(wd,gd_h))):
        gcp.append(pltpu.make_async_copy(a,b,gsem.at[j])); gcp[-1].start()
    tg_o[...]=jnp.zeros(tg_o.shape,f32)
    HH=Z*H
    dsf=bias.reshape(HH*R,SP) if False else bias
    U=16
    it=lax.broadcasted_iota(jnp.int32,(16,S),0).astype(jnp.int16)
    one=jnp.bfloat16(1); nil=jnp.bfloat16(0)
    def hist(q,_):
        hot=[]; grads=[]
        for u in range(U):
            i=q*U+u
            rows=bias[:,pl.ds(i,1),:].reshape(HH,SP)
            grads.append(jnp.concatenate([rows,jnp.zeros((16-HH,SP),f32)],axis=0).astype(bf)[:,:S])
            parts=[]
            for r,nb in ((i1,c.B1),(i2,c.B2),(i3,c.B2)):
                row=jnp.broadcast_to(r[pl.ds(i,1),:],(16,S)).astype(jnp.int16)
                for k in range(nb//16):
                    parts.append(jnp.where(row==it+jnp.int16(16*k),one,nil))
            hot.append(jnp.concatenate(parts,axis=0))
        tot=None
        for u in range(U):
            x=nt(grads[u],hot[u])
            tot=x if tot is None else tot+x
        tg_o[...]+=tot
        return 0
    lax.fori_loop(0,R//U,hist,0)
    for g in gcp: g.wait()

def scratch(c):
    R,SP,Z,H,HD,D,FZ=c.R,c.SP,c.Z,c.H,c.HD,c.D,c.FZ
    L=H*HD
    V=pltpu.VMEM
    return [V((Z,4*L,D),bf),V((Z,D,FZ),bf),V((Z,FZ,D),bf),pltpu.SemaphoreType.DMA((3,)),pltpu.SemaphoreType.DMA((3,)),V((Z*H,R,SP),f32),V((Z*H,R,SP),bf),V((Z,L,R),bf),V((Z,L,SP),bf),V((Z,L,SP),bf),V((Z,R,L),bf),
            V((R,D),f32),V((R,D),f32),V((R,128),f32),V((Z,R,FZ),bf),V((Z,R,FZ),bf),V((R,SP),bf),V((L,R),bf),V((R,D),f32),
            V((L,R),bf),V((2*L,SP),bf),V((R,D),bf),V((R,D),bf),V((R,D),f32)]
def outs(c):
    R,SP,Z,H,HD,D,FZ=c.R,c.SP,c.Z,c.H,c.HD,c.D,c.FZ
    L=H*HD; sd=jax.ShapeDtypeStruct
    return [sd((R,D),bf),sd((SP,D),f32),sd((Z,4*L,D),bf),sd((Z,D,FZ),bf),sd((Z,FZ,D),bf),sd((104,D),f32),sd((16,c.B1+2*c.B2),f32)]

def specs():
    v=pl.BlockSpec(memory_space=pltpu.VMEM); a=pl.BlockSpec(memory_space=pl.ANY)
    return [v]*6+[a]*3+[v]*4,[v,v,a,a,a,v,v]


def shards(hidden, qkv_weight, qv_bias, out_weight, out_bias, first_gain, first_shift, up_weight, up_bias,
           down_weight, down_bias, second_gain, second_shift, relative_table, horizontal_table, vertical_table,
           token_mask, relative_ids, horizontal_ids, vertical_ids, cotangent, NP=8, Z=4):
    c=Cfg()
    pages_here,sl,D=hidden.shape
    S=relative_ids.shape[1]
    c.R=S//2; c.S=S; c.SP=-(-S//128)*128; c.Z=Z; c.H=relative_table.shape[1]; c.D=D
    L=qkv_weight.shape[2]; c.HD=L//c.H; c.FZ=up_weight.shape[1]
    c.B1=relative_table.shape[0]; c.B2=horizontal_table.shape[0]
    g=lax.axis_index("pages"); z=lax.axis_index("heads"); k=g%2
    pairs=[[2*i,2*i+1] for i in range(NP//2)]
    swap=[(i,i^1) for i in range(NP)]
    def to_page(x):
        x=lax.all_gather(x,"pages",axis=0,tiled=True,axis_index_groups=pairs)
        return lax.all_to_all(x,"heads",split_axis=0,concat_axis=0,tiled=True).reshape(S,D)
    def from_page(x):
        x=lax.all_gather(x,"pages",axis=0,tiled=True,axis_index_groups=pairs).reshape(Z,sl,D)
        x=lax.all_to_all(x,"heads",split_axis=0,concat_axis=0,tiled=True)
        return lax.dynamic_slice_in_dim(x,k*pages_here,pages_here,0)
    xf=jnp.zeros((c.SP,D),bf).at[:S].set(to_page(hidden))
    ct=lax.dynamic_slice_in_dim(to_page(cotangent),k*c.R,c.R,0)
    owner=k==z//2
    def own_rows(x):
        page=lax.dynamic_index_in_dim(x,z%2,0,keepdims=False)
        mine=lax.dynamic_slice_in_dim(page,k*c.R,c.R,0)
        other=lax.ppermute(lax.dynamic_slice_in_dim(page,(1-k)*c.R,c.R,0),"pages",swap)
        return jnp.where(owner,mine,other)
    ids=[own_rows(x) for x in (relative_ids,horizontal_ids,vertical_ids)]
    mrow=lax.dynamic_index_in_dim(token_mask,z%2,0,keepdims=True)
    mrow=jnp.where(owner,mrow,lax.ppermute(mrow,"pages",swap)).astype(f32)
    mask=jnp.zeros((1,c.SP),f32).at[:,:S].set(mrow)
    wloc=jnp.stack([jnp.concatenate([qkv_weight.transpose(1,2,0).reshape(3*L,D),out_weight],0),up_weight,down_weight])
    e=D//8
    wl=lax.dynamic_slice_in_dim(wloc,(g%8)*e,e,1)
    wl=lax.all_gather(wl,"heads",axis=0)
    wl=lax.all_gather(wl,"pages",axis=0,axis_index_groups=[[8*i+j for j in range(8)] for i in range(NP//8)])
    W=wl.transpose(2,1,0,3,4).reshape(3,Z,D,D)
    qvb=lax.all_gather(qv_bias.astype(f32).reshape(1,2*L),"heads",axis=0,tiled=True)
    qvb=jnp.zeros((Z,8,2*L),f32).at[:,0].set(qvb)
    ub=lax.all_gather(up_bias.astype(f32)[None],"heads",axis=0,tiled=True)
    ub=jnp.zeros((Z,8,c.FZ),f32).at[:,0].set(ub)
    tb=jnp.zeros((3,c.H,128),f32)
    for t,x in enumerate((relative_table,horizontal_table,vertical_table)):
        tb=tb.at[t,:,:x.shape[0]].set(x.T.astype(f32))
    tb=lax.all_gather(tb,"heads",axis=1,tiled=True)
    tab=jnp.zeros((3,16,128),f32).at[:,:Z*c.H].set(tb)
    vec=jnp.stack([out_bias,first_gain,first_shift,down_bias,second_gain,second_shift,out_bias,out_bias]).astype(f32)
    kern=lambda *r: compute_kernel(c,lambda: pl.multiple_of((lax.axis_index("pages")%2)*c.R,16),*r)
    out,dh,ga,gu,gd,sm,tg=pl.pallas_call(kern,out_shape=outs(c),scratch_shapes=scratch(c),in_specs=specs()[0],out_specs=specs()[1],
        compiler_params=pltpu.CompilerParams(vmem_limit_bytes=67043328))(xf,ct,*ids,mask,W[0],W[1],W[2],qvb,ub,tab,vec)
    mine=lax.dynamic_slice_in_dim(dh,k*c.R,c.R,0)
    other=lax.ppermute(lax.dynamic_slice_in_dim(dh,(1-k)*c.R,c.R,0).astype(bf),"pages",swap)
    gh=from_page((mine+other.astype(f32)).astype(bf))
    o=from_page(out)
    G=jnp.stack([ga,gu,gd]).reshape(3,Z,NP,D//NP,D).transpose(2,1,0,3,4)
    G=lax.psum_scatter(G,"pages",scatter_dimension=0,tiled=False)
    G=lax.psum_scatter(G,"heads",scatter_dimension=0,tiled=False)
    G=lax.all_gather(G,"pages",axis=1,tiled=True).astype(f32)
    gq=G[0,:3*L].reshape(3,L,D).transpose(2,0,1)
    sm,tg=lax.psum((sm,tg),("pages","heads"))
    pick=lambda r0: lax.dynamic_index_in_dim(sm[r0:r0+8*Z].reshape(Z,8,D)[:,0],z,0,keepdims=False)
    gqv=jnp.stack([pick(40)[:L],pick(40+8*Z)[:L]])
    tl=lax.dynamic_slice_in_dim(tg,z*c.H,c.H,0).T
    return (o,gh,gq,gqv,G[0,3*L:],sm[0],sm[1],sm[2],G[1],pick(8),G[2],sm[3],sm[4],sm[5],tl[:c.B1],tl[c.B1:c.B1+c.B2],tl[c.B1+c.B2:])

def solution(mesh):
    in_specs = (
        P("pages", "heads", None),
        P(None, None, "heads"),
        P(None, "heads"),
        P("heads", None),
        P(),
        P(),
        P(),
        P(None, "heads"),
        P("heads"),
        P("heads", None),
        P(),
        P(),
        P(),
        P(None, "heads"),
        P(None, "heads"),
        P(None, "heads"),
        P("pages", None),
        P("pages", None, None),
        P("pages", None, None),
        P("pages", None, None),
        P("pages", "heads", None),
    )
    out_specs = (
        P("pages", "heads", None),
        P("pages", "heads", None),
        P(None, None, "heads"),
        P(None, "heads"),
        P("heads", None),
        P(),
        P(),
        P(),
        P(None, "heads"),
        P("heads"),
        P("heads", None),
        P(),
        P(),
        P(),
        P(None, "heads"),
        P(None, "heads"),
        P(None, "heads"),
    )
    f = lambda *a: shards(*a, NP=mesh.shape['pages'], Z=mesh.shape['heads'])
    return jax.shard_map(f, mesh=mesh, in_specs=in_specs, out_specs=out_specs, check_vma=False)
```

time: 1140 us -> 604 us (0.53)
  matrix products: 357 us -> 0 us
  local copies, waits for them, and re-layouts: 301 us -> 35.6 us
  Pallas kernels: 0 us -> 89 us
  blocking collectives: 65.9 us -> 107 us
  waiting for transfers between devices: 352 us -> 314 us
  starting transfers between devices: 0.84 us -> 15.9 us
    dot_general x58 -> x0, matrix products: 357 us -> none  [the longest x16 142 us: one_part(): jnp.dot(table_all, bucket_onehot(ids_piece, buckets), preferred_element_t...]
    reduce_scatter x0 -> x2, waiting for transfers between devices: none -> 141 us  [the longest x1 101 us: shards(): G = lax.psum_scatter(G, 'pages', scatter_dimension=0, tiled=False)]
    unnamed x13 -> x6, waiting for transfers between devices: 117 us -> 0.62 us
    slice x38 -> x11, local copies, waits for them, and re-layouts: 122 us -> 17.7 us  [the longest x2 8.52 us: shards(): W[2]]
    pallas_call x0 -> x1, Pallas kernels: none -> 89 us  [shards(): pl.pallas_call(kern, out_shape=outs(c), scratch_shapes=scratch(c), in_spe...]
    all_gather x4 -> x3, waiting for transfers between devices: 160 us -> 74.2 us  [the longest x1 43.1 us: shards(): wl = lax.all_gather(wl, 'heads', axis=0)]
    all_gather x0 -> x7, blocking collectives: none -> 63 us  [the longest x1 27 us: shards(): tb = lax.all_gather(tb, 'heads', axis=1, tiled=True)]
    reshape x10 -> x1, local copies, waits for them, and re-layouts: 61.6 us -> 1.01 us  [shards(): sm[r0:r0 + 8 * Z].reshape(Z, 8, D)[:, 0]]
  transfers between devices with their start and end apart: 9 -> 15, of which waited for: 8 -> 8; matrix products, arithmetic and copies ran while one was open for 2% -> 5% of each run, Pallas kernels for 0% -> 0%
where the time goes in v1:
time: 604 us; the launch traced here: 603 us
  waiting for transfers between devices  314 us (52%)
  blocking collectives  107 us (18%)
  Pallas kernels  89 us (15%)
  local copies, waits for them, and re-layouts  35.6 us (6%)
  other arithmetic  26.9 us (4%)
  starting transfers between devices  15.9 us (3%)
  between operations  14.6 us (2%)
    reduce_scatter x1, waiting for transfers between devices, shards(): G = lax.psum_scatter(G, 'pages', scatter_dimension=0, tiled=False)  101 us
    pallas_call x1, Pallas kernels, shards(): pl.pallas_call(kern, out_shape=outs(c), scratch_shapes=scratch(c), in_spe...  89 us
    psum x1, waiting for transfers between devices, shards(): sm, tg = lax.psum((sm, tg), ('pages', 'heads'))  64.1 us
    psum x1, blocking collectives, shards(): sm, tg = lax.psum((sm, tg), ('pages', 'heads'))  43.7 us
    all_gather x1, waiting for transfers between devices, shards(): wl = lax.all_gather(wl, 'heads', axis=0)  43.1 us
    reduce_scatter x1, waiting for transfers between devices, shards(): G = lax.psum_scatter(G, 'heads', scatter_dimension=0, tiled=False)  40.1 us
    all_gather x1, waiting for transfers between devices, shards(): G = lax.all_gather(G, 'pages', axis=1, tiled=True).astype(f32)  31.1 us
    all_gather x1, blocking collectives, shards(): tb = lax.all_gather(tb, 'heads', axis=1, tiled=True)  27 us
  transfers between devices with their start and end apart: 15, of which 8 were waited for; matrix products, arithmetic and copies ran while one was open for 5% of the time, Pallas kernels for 0%

profile of v1, /device:TPU:0, one launch (start us, length us, event | category | flops | bytes accessed | tf_op | source)
XLA Modules:
  0.0 602.7 jit_solution(14838365805182575396)
XLA Ops:
  7.3 1.3 maximum_bitcast_fusion
  8.6 1.8 fusion.1
  10.5 43.1 %all-gather.10.cloned.1.call-done = bf16[12,96,768]{2,1,0:T(8,128)(2,1)} async-done(((bf16[3,96,768]{2,1,0:T(8,128)(2,1)}), bf16[12,96,768]{2,1,0:T(8,128)(2,1)}) %all-gather.10.cloned.1.call-update) | async-done | bytes 1769488 | tf_op jit(solution)/shard_map/all_gather | solution.py:252
  53.6 2.6 all_gather.36
  56.2 3.6 all-to-all-start
  59.9 0.2 collective-permute-start.3
  60.1 2.2 dynamic-slice_bitcast_fusion
  62.4 0.4 collective-permute-start.2
  62.9 2.2 dynamic-slice_bitcast_fusion.1
  65.0 0.2 collective-permute-start.1
  65.2 2.1 dynamic-slice_bitcast_fusion.2
  67.3 0.4 collective-permute-start
  67.6 2.9 all_gather.37
  70.6 13.2 %all-to-all-done = bf16[4,152,768]{2,1,0:T(8,128)(2,1)S(1)} async-done(((bf16[4,152,768]{2,1,0:T(8,128)(2,1)}), bf16[4,152,768]{2,1,0:T(8,128)(2,1)S(1)}, u32[]{:S(2)}, u32[]{:S(2)}) %all-to-all-start) | async-done | bytes 933920 | tf_op jit(solution)/shard_map/all_to_all | solution.py:232
  83.7 3.5 all-to-all-start.1
  87.6 0.1 scatter.48
  87.8 0.1 scatter.49
  88.0 0.6 convert_element_type.36.r_12_
  88.6 27.0 %all_gather.44 = f32[3,12,128]{2,0,1:T(4,128)S(1)} all-gather(f32[3,3,128]{2,0,1:T(4,128)S(1)} %copy.50), channel_id=1, replica_groups=mesh['pages'=8,'heads'=4] {'heads'}, dimensions={1}, use_global_device_ids=true | all-gather | bytes 23040 | tf_op jit(solution)/shard_map/all_gather | solution.py:262
  115.6 0.6 scatter.50.r_11_
  116.2 13.1 %all-gather.5 = f32[4,1,768]{2,1,0:T(1,128)S(1)} all-gather(f32[1,1,768]{2,1,0:T(1,128)S(1)} %reshape.378), channel_id=4, replica_groups=mesh['pages'=8,'heads'=4] {'heads'}, dimensions={0}, use_global_device_ids=true | all-gather | bytes 15360 | tf_op jit(solution)/shard_map/all_gather | solution.py:257
  129.3 12.1 %all-gather.4 = f32[4,1,384]{2,1,0:T(1,128)S(1)} all-gather(f32[1,1,384]{2,1,0:T(1,128)S(1)} %reshape.376), channel_id=1, replica_groups=mesh['pages'=8,'heads'=4] {'heads'}, dimensions={0}, use_global_device_ids=true | all-gather | bytes 7680 | tf_op jit(solution)/shard_map/all_gather | solution.py:255
  141.4 0.6 scatter.34.r_9_
  142.1 0.6 scatter.35.r_10_
  142.7 0.6 compare_reduce_fusion
  143.3 0.7 broadcast_select_fusion.1
  144.0 0.6 scatter.31.r_5_
  144.6 2.1 bitcast_select_fusion.r_4_
  146.7 2.2 bitcast_select_fusion.1.r_3_
  148.9 2.1 bitcast_select_fusion.2.r_2_
  151.0 1.0 scatter.30.r_0_
  152.0 0.8 constant_dynamic-slice_fusion.7.r_1_
  152.8 5.9 fusion.7
  158.7 2.6 copy.49
  161.4 2.6 copy.48
  163.9 2.5 copy.47
  166.4 89.0 %shard_map.332 = (bf16[304,768]{1,0:T(8,128)(2,1)}, f32[640,768]{1,0:T(8,128)}, bf16[4,768,768]{2,1,0:T(8,128)(2,1)}, bf16[4,768,768]{2,1,0:T(8,128)(2,1)}, bf16...) custom-call(bf16[640,768]{1,0:T(8,128)(2,1)} %scatter.30.r_0_, ...), custom_call_target="tpu_custom_call" | custom-call | tf_op jit(solution)/shard_map/pallas_call | solution.py:266
  255.4 10.4 %copy_bitcast_fusion = bf16[8,4,3,96,768]{4,3,2,1,0:T(8,128)(2,1)} fusion(bf16[1,4,8,96,768]{4,3,2,1,0:T(8,128)(2,1)} %bitcast.76, bf16[1,4,8,96,768]{4,3,2,1,0:T(8,128)(2,1)} %bitcast.75, bf16[1,4,8,96,768]{4,3,2,1,0:T(8,128)(2,1)} %bitcast.74), kind=kLoop, calls=%fused_computation.1 | loop fusion | flops 14155776 | bytes 28311552 | tf_op jit(solution)/shard_map/transpose | solution.py:272
  265.9 100.9 %reduce-scatter.3.cloned.1.call-done = bf16[1,4,3,96,768]{4,3,2,1,0:T(8,128)(2,1)} async-done(((bf16[8,4,3,96,768]{4,3,2,1,0:T(8,128)(2,1)}), bf16[1,4,3,96,768]{4,3,2,1,0:T(8,128)(2,1)}) %reduce-scatter.3.cloned.1.call-update) | async-done | bytes 1769488 | tf_op jit(solution)/shard_map/reduce_scatter | solution.py:273
  366.9 0.5 all-reduce.8.cloned.1.call-update
  367.5 40.1 %reduce-scatter.5.cloned.1.call-done = bf16[1,3,96,768]{3,2,1,0:T(8,128)(2,1)} async-done(((bf16[4,3,96,768]{3,2,1,0:T(8,128)(2,1)}), bf16[1,3,96,768]{3,2,1,0:T(8,128)(2,1)}) %reduce-scatter.5.cloned.1.call-update) | async-done | bytes 442384 | tf_op jit(solution)/shard_map/reduce_scatter | solution.py:274
  407.5 2.6 all_gather.45
  410.2 3.6 all-to-all-start.2
  413.9 0.2 collective-permute-start.4
  414.1 1.8 collective-permute-done.4
  415.9 1.1 add_convert_fusion
  417.0 2.6 all_gather.46
  419.6 19.1 %all-to-all-done.2 = bf16[4,152,768]{2,1,0:T(8,128)(2,1)S(1)} async-done(((bf16[4,152,768]{2,1,0:T(8,128)(2,1)}), bf16[4,152,768]{2,1,0:T(8,128)(2,1)S(1)}, u32[]{:S(2)}, u32[]{:S(2)}) %all-to-all-start.2) | async-done | bytes 933920 | tf_op jit(solution)/shard_map/all_to_all | solution.py:235
  438.8 3.5 all-to-all-start.3
  442.3 43.7 %psum.15 = f32[16,160]{1,0:T(8,128)S(1)} all-reduce(f32[16,160]{1,0:T(8,128)S(1)} %copy-done.4), channel_id=1, replica_groups=mesh['pages'=8,'heads'=4] {'pages','heads'}, use_global_device_ids=true, to_apply=%region_4.5 | all-reduce | flops 2560 | bytes 20480 | tf_op jit(solution)/shard_map/psum | solution.py:277
  486.0 0.6 slice.286
  486.6 0.7 fusion.9
  487.3 64.1 %all-reduce.8.cloned.1.call-done = f32[104,768]{1,0:T(8,128)} async-done(((f32[104,768]{1,0:T(8,128)}), f32[104,768]{1,0:T(8,128)}) %all-reduce.8.cloned.1.call-update) | async-done | bytes 319504 | tf_op jit(solution)/shard_map/psum | solution.py:277
  551.4 1.0 slice_bitcast_fusion.3
  552.4 0.6 fusion.3
  553.1 0.6 pad_maximum_fusion.1
  553.6 1.6 slice_reduce_fusion
  555.3 0.8 constant_dynamic-slice_fusion.5
  556.1 0.8 constant_dynamic-slice_fusion.4
  556.9 31.1 %all-gather.14.cloned.1.call-done = bf16[1,3,768,768]{3,2,1,0:T(8,128)(2,1)} async-done(((bf16[1,3,96,768]{3,2,1,0:T(8,128)(2,1)}), bf16[1,3,768,768]{3,2,1,0:T(8,128)(2,1)}) %all-gather.14.cloned.1.call-update) | async-done | bytes 3538960 | tf_op jit(solution)/shard_map/all_gather | solution.py:275
  588.0 3.2 fusion.8
  591.2 0.9 slice_bitcast_fusion.2
  592.0 1.3 slice.270
  593.4 2.5 slice_bitcast_fusion
  (73 shorter events, 0.7 us)
Async XLA Ops:
  7.2 46.4 %all-gather.10.cloned.1.call-start = ((), (), s32[]{:S(2)}) async-start(), calls=%async_computation.9 | async-start | bytes 2211840 | tf_op jit(solution)/shard_map/all_gather | solution.py:252
  8.6 45.0 %copy-start.1 = (bf16[2,152,768]{2,1,0:T(8,128)(2,1)S(1)}, bf16[2,152,768]{2,1,0:T(8,128)(2,1)}, u32[]{:S(2)}) copy-start(bf16[2,152,768]{2,1,0:T(8,128)(2,1)} %param.37) | copy-start | bytes 1400836
  10.4 49.5 %copy-start.5 = (s32[2,608]{1,0:T(2,128)S(1)}, s32[2,608]{1,0:T(2,128)}, u32[]{:S(2)}) copy-start(s32[2,608]{1,0:T(2,128)} %param.53) | copy-start | bytes 14596
  10.5 142.4 %all-gather.12.cloned.1.call-start = ((), (), s32[]{:S(2)}) async-start(), calls=%async_computation.10 | async-start | bytes 15925248 | tf_op jit(solution)/shard_map/all_gather | solution.py:253
  56.2 11.4 %copy-start.2 = (bf16[2,152,768]{2,1,0:T(8,128)(2,1)S(1)}, bf16[2,152,768]{2,1,0:T(8,128)(2,1)}, u32[]{:S(2)}) copy-start(bf16[2,152,768]{2,1,0:T(8,128)(2,1)} %param.57) | copy-start | bytes 1400836
  56.2 27.5 %all-to-all-start = ((bf16[4,152,768]{2,1,0:T(8,128)(2,1)}), bf16[4,152,768]{2,1,0:T(8,128)(2,1)S(1)}, u32[]{:S(2)}, u32[]{:S(2)}) async-start(bf16[4,152,768]{2,1,0:T(8,128)(2,1)} %all_gather.36), calls=%async_computation | async-start | bytes 1867776 | tf_op jit(solution)/shard_map/all_to_all | solution.py:232
  59.9 83.4 %collective-permute-start.3 = (s32[1,608]{1,0:T(1,128)S(1)}, s32[1,608]{1,0:T(1,128)S(1)}, u32[]{:S(2)}, u32[]{:S(2)}) collective-permute-start(s32[1,608]{1,0:T(1,128)S(1)} %constant_dynamic-slice_fusion.6), channel_id=1, source_target_pairs={{0,4},{4,0},{8,12},{12,8},{16,20},{20,16},{24,28},{28,24},{1,5},{5... | collective-permute-start | bytes 7304 | tf_op jit(solution)/shard_map/ppermute | solution.py:247
  62.3 24.9 %copy-start.13 = (bf16[64,3]{0,1:T(4,128)(2,1)S(1)}, bf16[64,3]{0,1:T(4,128)(2,1)}, u32[]{:S(2)}) copy-start(bf16[64,3]{0,1:T(4,128)(2,1)} %param.51) | copy-start | bytes 1156
  62.3 25.0 %copy-start.14 = (bf16[32,3]{0,1:T(4,128)(2,1)S(1)}, bf16[32,3]{0,1:T(4,128)(2,1)}, u32[]{:S(2)}) copy-start(bf16[32,3]{0,1:T(4,128)(2,1)} %param.50) | copy-start | bytes 580
  62.3 25.0 %copy-start.16 = (bf16[2,192]{1,0:T(2,128)(2,1)S(1)}, bf16[2,192]{1,0:T(2,128)(2,1)}, u32[]{:S(2)}) copy-start(bf16[2,192]{1,0:T(2,128)(2,1)} %param.39) | copy-start | bytes 2308
  62.3 25.1 %copy-start.6 = (bf16[768]{0:T(1024)(128)(2,1)S(1)}, bf16[768]{0:T(1024)(128)(2,1)}, u32[]{:S(2)}) copy-start(bf16[768]{0:T(1024)(128)(2,1)} %param.41) | copy-start | bytes 4612
  62.3 25.1 %copy-start.7 = (bf16[768]{0:T(1024)(128)(2,1)S(1)}, bf16[768]{0:T(1024)(128)(2,1)}, u32[]{:S(2)}) copy-start(bf16[768]{0:T(1024)(128)(2,1)} %param.42) | copy-start | bytes 4612
  62.4 25.1 %copy-start.8 = (bf16[768]{0:T(1024)(128)(2,1)S(1)}, bf16[768]{0:T(1024)(128)(2,1)}, u32[]{:S(2)}) copy-start(bf16[768]{0:T(1024)(128)(2,1)} %param.43) | copy-start | bytes 4612
  62.4 25.1 %copy-start.9 = (bf16[768]{0:T(1024)(128)(2,1)S(1)}, bf16[768]{0:T(1024)(128)(2,1)}, u32[]{:S(2)}) copy-start(bf16[768]{0:T(1024)(128)(2,1)} %param.45) | copy-start | bytes 4612
  62.4 25.1 %copy-start.10 = (bf16[768]{0:T(1024)(128)(2,1)S(1)}, bf16[768]{0:T(1024)(128)(2,1)}, u32[]{:S(2)}) copy-start(bf16[768]{0:T(1024)(128)(2,1)} %param.47) | copy-start | bytes 4612
  62.4 25.2 %copy-start.11 = (bf16[768]{0:T(1024)(128)(2,1)S(1)}, bf16[768]{0:T(1024)(128)(2,1)}, u32[]{:S(2)}) copy-start(bf16[768]{0:T(1024)(128)(2,1)} %param.48) | copy-start | bytes 4612
  62.4 25.2 %copy-start.12 = (bf16[768]{0:T(1024)(128)(2,1)S(1)}, bf16[768]{0:T(1024)(128)(2,1)}, u32[]{:S(2)}) copy-start(bf16[768]{0:T(1024)(128)(2,1)} %param.49) | copy-start | bytes 4612
  62.4 25.3 %copy-start.15 = (bf16[64,3]{0,1:T(4,128)(2,1)S(1)}, bf16[64,3]{0,1:T(4,128)(2,1)}, u32[]{:S(2)}) copy-start(bf16[64,3]{0,1:T(4,128)(2,1)} %param.52) | copy-start | bytes 1156
  62.4 82.2 %collective-permute-start.2 = (s32[304,608]{1,0:T(8,128)}, s32[304,608]{1,0:T(8,128)}, u32[]{:S(2)}, u32[]{:S(2)}) collective-permute-start(s32[304,608]{1,0:T(8,128)} %dynamic-slice_bitcast_fusion), channel_id=1, source_target_pairs={{0,4},{4,0},{8,12},{12,8},{16,20},{20,16},{24,28},{28,24},{1,5},{5... | collective-permute-start | bytes 2217992 | tf_op jit(solution)/shard_map/ppermute | solution.py:243
  65.0 81.7 %collective-permute-start.1 = (s32[304,608]{1,0:T(8,128)}, s32[304,608]{1,0:T(8,128)S(1)}, u32[]{:S(2)}, u32[]{:S(2)}) collective-permute-start(s32[304,608]{1,0:T(8,128)} %dynamic-slice_bitcast_fusion.1), channel_id=1, source_target_pairs={{0,4},{4,0},{8,12},{12,8},{16,20},{20,16},{24,28},{28,24},{1,5},{5... | collective-permute-start | bytes 2217992 | tf_op jit(solution)/shard_map/ppermute | solution.py:243
  67.3 81.6 %collective-permute-start = (s32[304,608]{1,0:T(8,128)}, s32[304,608]{1,0:T(8,128)S(1)}, u32[]{:S(2)}, u32[]{:S(2)}) collective-permute-start(s32[304,608]{1,0:T(8,128)} %dynamic-slice_bitcast_fusion.2), channel_id=1, source_target_pairs={{0,4},{4,0},{8,12},{12,8},{16,20},{20,16},{24,28},{28,24},{1,5},{5... | collective-permute-start | bytes 2217992 | tf_op jit(solution)/shard_map/ppermute | solution.py:243
  83.7 68.3 %all-to-all-start.1 = ((bf16[4,152,768]{2,1,0:T(8,128)(2,1)}), bf16[4,152,768]{2,1,0:T(8,128)(2,1)S(1)}, u32[]{:S(2)}, u32[]{:S(2)}) async-start(bf16[4,152,768]{2,1,0:T(8,128)(2,1)} %all_gather.37), calls=%async_computation.1 | async-start | bytes 1867776 | tf_op jit(solution)/shard_map/all_to_all | solution.py:232
  87.2 279.6 %reduce-scatter.3.cloned.1.call-start = ((), (), s32[]{:S(2)}) async-start(), calls=%async_computation.6 | async-start | bytes 15925248 | tf_op jit(solution)/shard_map/reduce_scatter | solution.py:273
  265.9 141.7 %copy-start.3 = (bf16[304,768]{1,0:T(8,128)(2,1)S(1)}, bf16[304,768]{1,0:T(8,128)(2,1)}, u32[]{:S(2)}) copy-start(bf16[304,768]{1,0:T(8,128)(2,1)} %get-tuple-element.120) | copy-start | bytes 1400836
  265.9 147.9 %copy-start = (f32[640,768]{1,0:T(8,128)S(1)}, f32[640,768]{1,0:T(8,128)}, u32[]{:S(2)}) copy-start(f32[640,768]{1,0:T(8,128)} %get-tuple-element.121) | copy-start | bytes 5898244
  265.9 141.6 %reduce-scatter.5.cloned.1.call-start = ((), (), s32[]{:S(2)}) async-start(), calls=%async_computation.7 | async-start | bytes 2211840 | tf_op jit(solution)/shard_map/reduce_scatter | solution.py:274
  366.8 184.6 %all-reduce.8.cloned.1.call-start = ((), (), s32[]{:S(2)}) async-start(), calls=%async_computation.8 | async-start | bytes 638976 | tf_op jit(solution)/shard_map/psum | solution.py:277
  367.4 220.5 %all-gather.14.cloned.1.call-start = ((), (), s32[]{:S(2)}) async-start(), calls=%async_computation.11 | async-start | bytes 3981312 | tf_op jit(solution)/shard_map/all_gather | solution.py:275
  410.2 32.1 %copy-start.4 = (f32[16,160]{1,0:T(8,128)S(1)}, f32[16,160]{1,0:T(8,128)}, u32[]{:S(2)}) copy-start(f32[16,160]{1,0:T(8,128)} %get-tuple-element.126) | copy-start | bytes 30724
  410.2 28.6 %all-to-all-start.2 = ((bf16[4,152,768]{2,1,0:T(8,128)(2,1)}), bf16[4,152,768]{2,1,0:T(8,128)(2,1)S(1)}, u32[]{:S(2)}, u32[]{:S(2)}) async-start(bf16[4,152,768]{2,1,0:T(8,128)(2,1)} %bitcast.26), calls=%async_computation.2 | async-start | bytes 1867776 | tf_op jit(solution)/shard_map/all_to_all | solution.py:235
  413.9 2.0 collective-permute-start.4
  438.8 117.3 %all-to-all-start.3 = ((bf16[4,152,768]{2,1,0:T(8,128)(2,1)}), bf16[4,152,768]{2,1,0:T(8,128)(2,1)S(1)}, u32[]{:S(2)}, u32[]{:S(2)}) async-start(bf16[4,152,768]{2,1,0:T(8,128)(2,1)} %bitcast.27), calls=%async_computation.3 | async-start | bytes 1867776 | tf_op jit(solution)/shard_map/all_to_all | solution.py:235
Sparse Core Ops, SparseCore 0:
  10.6 42.9 all-gather.9
  55.5 77.5 all-gather.11
  266.0 100.7 reduce-scatter.2
  369.0 38.4 reduce-scatter.4
  413.3 138.0 all-reduce.7
  553.1 34.7 all-gather.13
